TPU v7x, 256 devices: a whole 4x4x8 slice. The times are simulated.
256 devices in a mesh: tm: 8 (over x_hi, y), azim: 32 (over z, x_lo, core).
Axes of the slice: x: 4 (x_hi: 2, x_lo: 2; x = x_hi * 2 + x_lo), y: 4, z: 8, core: 2. Of those that a mesh axis runs over, the one named last changes fastest.
Arguments:
- rotor_coeffs: float32 [64, 2, 32, 16384], P('tm', None, 'azim'), may hold values from -1.5 to 1.5
- mortar_weights: float32 [64, 2, 32, 16384], P('tm', None, 'azim'), may hold values from 0.2 to 1
- block_shifts: int32 [64], P('tm'), may hold values from 0 to 31
- stencil_offsets: int32 [64, 2], P('tm'), may hold values from -1 to 1
- reluctivity: float32 [32, 16384], P('azim'), may hold values from 0.5 to 2
- source: float32 [64, 2, 32, 16384], P('tm', None, 'azim'), may hold values from -3 to 3
Outputs:
- residual: float32 [64, 2, 32, 16384], P('tm', None, 'azim')
All inputs are finite; a program needn't handle non-finite values.
Results may differ from a plain program's by a relative error of at most 0.0001.
Values sent between devices are 32-bit elements; how exact they have to be, the bound alone decides.
A program may use at most 128 MiB of HBM per device.

v0:
```python
import itertools
import jax
import jax.numpy as jnp
import numpy as np
from jax import lax
from jax.sharding import PartitionSpec as P

KC = 64
NT = 64
LANES = 128


def shifted(value, axis, steps):
    count = lax.axis_size(axis)
    pairs = [(source, (source + steps) % count) for source in range(count)]
    return lax.ppermute(value, axis, pairs)


def harmonic_basis(sample_rows, coefficient_count):
    column = jnp.arange(coefficient_count, dtype=jnp.int32)
    harmonic_order = 2 * (column // 2) + 1
    phase_index = harmonic_order[None, :] * (2 * sample_rows[:, None] + 1) % (4 * NT)
    phase_angle = phase_index.astype(jnp.float32) * (jnp.pi / (2 * NT))
    return jnp.where(column[None, :] % 2 == 0, jnp.cos(phase_angle), jnp.sin(phase_angle))


def per_sample(flags, value):
    return flags.reshape((-1,) + (1,) * (value.ndim - 1))


def digit_table(stages, count):
    found = {}
    for bits in itertools.product((0, 1), repeat=len(stages)):
        found.setdefault(sum((b * s for b, s in zip(bits, stages))) % count, bits)
    return np.array([found[d] for d in range(count)], np.int32)


def barrel(value, amounts, stages, axis):
    count = lax.axis_size(axis)
    picks = jnp.take(jnp.asarray(digit_table(stages, count)), amounts % count, axis=0)
    for level, steps in enumerate(stages):
        moved = shifted(value, axis, steps)
        value = jnp.where(per_sample(picks[:, level] == 1, value), moved, value)
    return value


def body(rotor_coeffs, mortar_weights, block_shifts, stencil_offsets, reluctivity, source):
    local_c, comp, _, nodes = rotor_coeffs.shape
    local_j, sten = mortar_weights.shape[:2]
    rows = nodes // LANES
    parts = lax.axis_size("tm")
    chunk = rows // parts
    coeffs = lax.all_to_all(
        rotor_coeffs.reshape(local_c, comp, rows, LANES),
        "tm",
        split_axis=2,
        concat_axis=0,
        tiled=True,
    )
    weights = lax.all_to_all(
        mortar_weights.reshape(local_j, sten, rows, LANES),
        "tm",
        split_axis=2,
        concat_axis=0,
        tiled=True,
    )
    small = jnp.concatenate([block_shifts[:, None], stencil_offsets], axis=1).astype(jnp.float32)
    small = lax.all_gather(small, "tm", tiled=True).astype(jnp.int32)
    shifts, offsets = (small[:, 0], small[:, 1:])
    gain = lax.dynamic_slice_in_dim(
        reluctivity.reshape(rows, LANES), lax.axis_index("tm") * chunk, chunk, axis=0
    )
    table = harmonic_basis(jnp.arange(NT, dtype=jnp.int32), KC)
    samples = jnp.einsum("jc,capk->japk", table, coeffs, precision=lax.Precision.HIGHEST)
    orders = ((1, 2, 4, -8, 16), (16, 8, -4, 2, 1))
    fields = []
    for component in range(comp):
        turned = barrel(samples[:, component], shifts, orders[component % 2], "azim")
        from_left = shifted(turned, "azim", 1)
        from_right = shifted(turned, "azim", -1)
        field = jnp.zeros_like(turned)
        for stencil_entry in range(sten):
            offset = offsets[:, stencil_entry]
            neighbour = jnp.where(
                per_sample(offset == 0, turned),
                turned,
                jnp.where(per_sample(offset > 0, turned), from_right, from_left),
            )
            field = field + weights[:, stencil_entry] * neighbour
        fields.append(field)
    airgap_field = jnp.stack(fields, axis=1)
    square = jnp.sum(airgap_field * airgap_field, axis=1, keepdims=True)
    field_flux = gain[None, None] * (1.0 + square / (1.0 + square)) * airgap_field
    summed = jnp.einsum(
        "jc,japk->capk", table * (2.0 / NT), field_flux, precision=lax.Precision.HIGHEST
    )
    residual = lax.all_to_all(summed, "tm", split_axis=0, concat_axis=2, tiled=True)
    return residual.reshape(source.shape) - source


def solution(mesh):
    in_specs = (
        P("tm", None, "azim", None),
        P("tm", None, "azim", None),
        P("tm"),
        P("tm", None),
        P("azim", None),
        P("tm", None, "azim", None),
    )
    out_specs = P("tm", None, "azim", None)
    return jax.shard_map(body, mesh=mesh, in_specs=in_specs, out_specs=out_specs, check_vma=False)
```

profile of v0, /device:TPU:1, one launch (start us, length us, event | category | flops | bytes accessed | tf_op | source)
XLA Modules:
  0.0 249.5 jit_solution(8012935296902372771)
XLA Ops:
  0.0 3.0 %copy.42 = f32[8,2,128,128]{3,1,0,2:T(2,128)} copy(f32[8,2,128,128]{3,2,1,0:T(8,128)} %bitcast.73) | data formatting | bytes 2097152 | tf_op jit(solution)/shard_map/reshape | solution.py:54
  3.0 7.5 %all-to-all-start.1 = ((f32[8,2,128,128]{3,1,0,2:T(2,128)}), f32[8,2,128,128]{3,1,0,2:T(2,128)S(1)}, u32[]{:S(2)}, u32[]{:S(2)}) async-start(f32[8,2,128,128]{3,1,0,2:T(2,128)} %copy.42), calls=%async_computation.1 | async-start | bytes 2097152 | tf_op jit(solution)/shard_map/all_to_all | solution.py:53
  11.2 34.0 %all-gather = f32[8,8,3]{1,2,0:T(4,128)S(1)} all-gather(f32[1,8,3]{1,2,0:T(4,128)S(1)} %fusion.25), channel_id=1, replica_groups=mesh['tm'=8,'azim'=32] {'tm'}, dimensions={0}, use_global_device_ids=true | all-gather | bytes 864 | tf_op jit(solution)/shard_map/all_gather | solution.py:68
  45.7 1.8 fusion
  47.6 5.6 %collective-permute-start = (f32[64,16,128]{2,0,1:T(8,128)S(1)}, f32[64,16,128]{2,0,1:T(8,128)S(1)}, u32[]{:S(2)}, u32[]{:S(2)}) collective-permute-start(f32[64,16,128]{2,0,1:T(8,128)S(1)} %get-tuple-element.22), channel_id=1, source_target_pairs={{0,1},{1,2},{2,3},{3,4},{4,5},{5,6},{6,7},{7,8},{8,9},{9,10},{10,1... | collective-permute-start | bytes 1572872 | tf_op jit(solution)/shard_map/ppermute | solution.py:16
  53.2 6.9 %collective-permute-start.7 = (f32[64,16,128]{2,0,1:T(8,128)S(1)}, f32[64,16,128]{2,0,1:T(8,128)S(1)}, u32[]{:S(2)}, u32[]{:S(2)}) collective-permute-start(f32[64,16,128]{2,0,1:T(8,128)S(1)} %get-tuple-element.23), channel_id=1, source_target_pairs={{0,16},{1,17},{2,18},{3,19},{4,20},{5,21},{6,22},{7,23},{8,24},{9,... | collective-permute-start | bytes 1572872 | tf_op jit(solution)/shard_map/ppermute | solution.py:16
  62.0 12.7 %collective-permute-done.7 = f32[64,16,128]{2,0,1:T(8,128)S(1)} collective-permute-done((f32[64,16,128]{2,0,1:T(8,128)S(1)}, f32[64,16,128]{2,0,1:T(8,128)S(1)}, u32[]{:S(2)}, u32[]{:S(2)}) %collective-permute-start.7) | collective-permute-done | bytes 524320 | tf_op jit(solution)/shard_map/ppermute | solution.py:16
  74.9 7.1 %collective-permute-start.1 = (f32[64,16,128]{2,0,1:T(8,128)S(1)}, f32[64,16,128]{2,0,1:T(8,128)S(1)}, u32[]{:S(2)}, u32[]{:S(2)}) collective-permute-start(f32[64,16,128]{2,0,1:T(8,128)S(1)} %get-tuple-element.20), channel_id=1, source_target_pairs={{0,2},{1,3},{2,4},{3,5},{4,6},{5,7},{6,8},{7,9},{8,10},{9,11},{10,... | collective-permute-start | bytes 1572872 | tf_op jit(solution)/shard_map/ppermute | solution.py:16
  82.0 9.7 %collective-permute-start.8 = (f32[64,16,128]{2,0,1:T(8,128)S(1)}, f32[64,16,128]{2,0,1:T(8,128)S(1)}, u32[]{:S(2)}, u32[]{:S(2)}) collective-permute-start(f32[64,16,128]{2,0,1:T(8,128)S(1)} %get-tuple-element.21), channel_id=1, source_target_pairs={{0,8},{1,9},{2,10},{3,11},{4,12},{5,13},{6,14},{7,15},{8,16},{9,17... | collective-permute-start | bytes 1572872 | tf_op jit(solution)/shard_map/ppermute | solution.py:16
  91.7 8.9 %collective-permute-done.1 = f32[64,16,128]{2,0,1:T(8,128)S(1)} collective-permute-done((f32[64,16,128]{2,0,1:T(8,128)S(1)}, f32[64,16,128]{2,0,1:T(8,128)S(1)}, u32[]{:S(2)}, u32[]{:S(2)}) %collective-permute-start.1) | collective-permute-done | bytes 524320 | tf_op jit(solution)/shard_map/ppermute | solution.py:16
  100.7 1.0 collective-permute-start.2
  101.8 11.3 %collective-permute-done.8 = f32[64,16,128]{2,0,1:T(8,128)S(1)} collective-permute-done((f32[64,16,128]{2,0,1:T(8,128)S(1)}, f32[64,16,128]{2,0,1:T(8,128)S(1)}, u32[]{:S(2)}, u32[]{:S(2)}) %collective-permute-start.8) | collective-permute-done | bytes 524320 | tf_op jit(solution)/shard_map/ppermute | solution.py:16
  113.3 11.0 %collective-permute-done.2 = f32[64,16,128]{2,0,1:T(8,128)S(1)} collective-permute-done((f32[64,16,128]{2,0,1:T(8,128)S(1)}, f32[64,16,128]{2,0,1:T(8,128)S(1)}, u32[]{:S(2)}, u32[]{:S(2)}) %collective-permute-start.2) | collective-permute-done | bytes 524320 | tf_op jit(solution)/shard_map/ppermute | solution.py:16
  126.5 10.6 %collective-permute-start.10 = (f32[64,16,128]{2,0,1:T(8,128)S(1)}, f32[64,16,128]{2,0,1:T(8,128)S(1)}, u32[]{:S(2)}, u32[]{:S(2)}) collective-permute-start(f32[64,16,128]{2,0,1:T(8,128)S(1)} %broadcast_select_fusion.2), channel_id=1, source_target_pairs={{0,2},{1,3},{2,4},{3,5},{4,6},{5,7},{6,8},{7,9},{8,10},{9,11},{10,... | collective-permute-start | bytes 1572872 | tf_op jit(solution)/shard_map/ppermute | solution.py:16
  137.1 12.8 %collective-permute-done.3 = f32[64,16,128]{2,0,1:T(8,128)S(1)} collective-permute-done((f32[64,16,128]{2,0,1:T(8,128)S(1)}, f32[64,16,128]{2,0,1:T(8,128)S(1)}, u32[]{:S(2)}, u32[]{:S(2)}) %collective-permute-start.3) | collective-permute-done | bytes 524320 | tf_op jit(solution)/shard_map/ppermute | solution.py:16
  150.0 2.1 collective-permute-start.4
  152.3 26.2 %collective-permute-start.11 = (f32[64,16,128]{2,0,1:T(8,128)S(1)}, f32[64,16,128]{2,0,1:T(8,128)}, u32[]{:S(2)}, u32[]{:S(2)}) collective-permute-start(f32[64,16,128]{2,0,1:T(8,128)S(1)} %broadcast_select_fusion.3), channel_id=1, source_target_pairs={{0,1},{1,2},{2,3},{3,4},{4,5},{5,6},{6,7},{7,8},{8,9},{9,10},{10,1... | collective-permute-start | bytes 1572872 | tf_op jit(solution)/shard_map/ppermute | solution.py:16
  178.5 1.8 copy.37
  180.3 3.6 %all-to-all-start = ((f32[8,2,128,128]{3,1,0,2:T(2,128)}), f32[8,2,128,128]{3,1,0,2:T(2,128)S(1)}, u32[]{:S(2)}, u32[]{:S(2)}) async-start(f32[8,2,128,128]{3,1,0,2:T(2,128)} %copy.37), calls=%async_computation | async-start | bytes 2097152 | tf_op jit(solution)/shard_map/all_to_all | solution.py:60
  184.0 1.7 collective-permute-start.5
  185.7 7.0 %collective-permute-start.6 = (f32[64,16,128]{2,0,1:T(8,128)S(1)}, f32[64,16,128]{2,0,1:T(8,128)}, u32[]{:S(2)}, u32[]{:S(2)}) collective-permute-start(f32[64,16,128]{2,0,1:T(8,128)S(1)} %broadcast_select_fusion.9), channel_id=1, source_target_pairs={{0,1},{1,2},{2,3},{3,4},{4,5},{5,6},{6,7},{7,8},{8,9},{9,10},{10,1... | collective-permute-start | bytes 1572872 | tf_op jit(solution)/shard_map/ppermute | solution.py:16
  192.7 1.3 collective-permute-done.11
  194.0 1.2 broadcast_select_fusion.4
  195.1 5.5 %collective-permute-start.12 = (f32[64,16,128]{2,0,1:T(8,128)S(1)}, f32[64,16,128]{2,0,1:T(8,128)S(1)}, u32[]{:S(2)}, u32[]{:S(2)}) collective-permute-start(f32[64,16,128]{2,0,1:T(8,128)S(1)} %broadcast_select_fusion.4), channel_id=1, source_target_pairs={{0,31},{1,0},{2,1},{3,2},{4,3},{5,4},{6,5},{7,6},{8,7},{9,8},{10,9... | collective-permute-start | bytes 1572872 | tf_op jit(solution)/shard_map/ppermute | solution.py:16
  200.6 5.0 %all-to-all-done = f32[8,2,128,128]{3,1,0,2:T(2,128)S(1)} async-done(((f32[8,2,128,128]{3,1,0,2:T(2,128)}), f32[8,2,128,128]{3,1,0,2:T(2,128)S(1)}, u32[]{:S(2)}, u32[]{:S(2)}) %all-to-all-start) | async-done | bytes 1048608 | tf_op jit(solution)/shard_map/all_to_all | solution.py:60
  206.6 9.3 %collective-permute-done.5 = f32[64,16,128]{2,0,1:T(8,128)S(1)} collective-permute-done((f32[64,16,128]{2,0,1:T(8,128)S(1)}, f32[64,16,128]{2,0,1:T(8,128)S(1)}, u32[]{:S(2)}, u32[]{:S(2)}) %collective-permute-start.5) | collective-permute-done | bytes 524320 | tf_op jit(solution)/shard_map/ppermute | solution.py:16
  215.9 10.1 %collective-permute-done.12 = f32[64,16,128]{2,0,1:T(8,128)S(1)} collective-permute-done((f32[64,16,128]{2,0,1:T(8,128)S(1)}, f32[64,16,128]{2,0,1:T(8,128)S(1)}, u32[]{:S(2)}, u32[]{:S(2)}) %collective-permute-start.12) | collective-permute-done | bytes 524320 | tf_op jit(solution)/shard_map/ppermute | solution.py:16
  226.0 1.7 add_bitcast_fusion.1
  227.9 1.2 fusion.3
  229.8 16.5 %all_to_all.51 = f32[64,2,16,128]{3,2,1,0:T(8,128)S(1)} all-to-all(f32[64,2,16,128]{3,2,1,0:T(8,128)S(1)} %copy.46), channel_id=1, replica_groups=mesh['tm'=8,'azim'=32] {'tm'}, dimensions={0} | all-to-all | bytes 2097152 | tf_op jit(solution)/shard_map/all_to_all | solution.py:97
  246.3 1.1 copy-done.3
  247.5 2.1 sub.12
  (52 shorter events, 8.0 us)
Async XLA Ops:
  0.0 200.6 %copy-start = (f32[1,16384]{1,0:T(1,128)S(1)}, f32[1,16384]{1,0:T(1,128)}, u32[]{:S(2)}) copy-start(f32[1,16384]{1,0:T(1,128)} %param.14) | copy-start | bytes 196612
  3.0 42.3 %all-to-all-start.1 = ((f32[8,2,128,128]{3,1,0,2:T(2,128)}), f32[8,2,128,128]{3,1,0,2:T(2,128)S(1)}, u32[]{:S(2)}, u32[]{:S(2)}) async-start(f32[8,2,128,128]{3,1,0,2:T(2,128)} %copy.42), calls=%async_computation.1 | async-start | bytes 2097152 | tf_op jit(solution)/shard_map/all_to_all | solution.py:53
  10.5 0.7 copy-start.5
  10.5 0.7 copy-start.6
  47.5 12.7 %copy-start.1 = (s32[32,5]{1,0:T(8,128)S(1)}, s32[32,5]{1,0:T(8,128)}, u32[]{:S(2)}) copy-start(s32[32,5]{1,0:T(8,128)} %constant.99.clone2.1) | copy-start | bytes 1924
  47.6 14.4 %collective-permute-start = (f32[64,16,128]{2,0,1:T(8,128)S(1)}, f32[64,16,128]{2,0,1:T(8,128)S(1)}, u32[]{:S(2)}, u32[]{:S(2)}) collective-permute-start(f32[64,16,128]{2,0,1:T(8,128)S(1)} %get-tuple-element.22), channel_id=1, source_target_pairs={{0,1},{1,2},{2,3},{3,4},{4,5},{5,6},{6,7},{7,8},{8,9},{9,10},{10,1... | collective-permute-start | bytes 1572872 | tf_op jit(solution)/shard_map/ppermute | solution.py:16
  53.2 21.5 %collective-permute-start.7 = (f32[64,16,128]{2,0,1:T(8,128)S(1)}, f32[64,16,128]{2,0,1:T(8,128)S(1)}, u32[]{:S(2)}, u32[]{:S(2)}) collective-permute-start(f32[64,16,128]{2,0,1:T(8,128)S(1)} %get-tuple-element.23), channel_id=1, source_target_pairs={{0,16},{1,17},{2,18},{3,19},{4,20},{5,21},{6,22},{7,23},{8,24},{9,... | collective-permute-start | bytes 1572872 | tf_op jit(solution)/shard_map/ppermute | solution.py:16
  60.2 0.7 copy-start.2
  74.9 25.7 %collective-permute-start.1 = (f32[64,16,128]{2,0,1:T(8,128)S(1)}, f32[64,16,128]{2,0,1:T(8,128)S(1)}, u32[]{:S(2)}, u32[]{:S(2)}) collective-permute-start(f32[64,16,128]{2,0,1:T(8,128)S(1)} %get-tuple-element.20), channel_id=1, source_target_pairs={{0,2},{1,3},{2,4},{3,5},{4,6},{5,7},{6,8},{7,9},{8,10},{9,11},{10,... | collective-permute-start | bytes 1572872 | tf_op jit(solution)/shard_map/ppermute | solution.py:16
  82.0 31.1 %collective-permute-start.8 = (f32[64,16,128]{2,0,1:T(8,128)S(1)}, f32[64,16,128]{2,0,1:T(8,128)S(1)}, u32[]{:S(2)}, u32[]{:S(2)}) collective-permute-start(f32[64,16,128]{2,0,1:T(8,128)S(1)} %get-tuple-element.21), channel_id=1, source_target_pairs={{0,8},{1,9},{2,10},{3,11},{4,12},{5,13},{6,14},{7,15},{8,16},{9,17... | collective-permute-start | bytes 1572872 | tf_op jit(solution)/shard_map/ppermute | solution.py:16
  100.7 23.6 %collective-permute-start.2 = (f32[64,16,128]{2,0,1:T(8,128)S(1)}, f32[64,16,128]{2,0,1:T(8,128)S(1)}, u32[]{:S(2)}, u32[]{:S(2)}) collective-permute-start(f32[64,16,128]{2,0,1:T(8,128)S(1)} %broadcast_select_fusion.6), channel_id=1, source_target_pairs={{0,4},{1,5},{2,6},{3,7},{4,8},{5,9},{6,10},{7,11},{8,12},{9,13},{1... | collective-permute-start | bytes 1572872 | tf_op jit(solution)/shard_map/ppermute | solution.py:16
  113.2 13.1 %collective-permute-start.9 = (f32[64,16,128]{2,0,1:T(8,128)S(1)}, f32[64,16,128]{2,0,1:T(8,128)S(1)}, u32[]{:S(2)}, u32[]{:S(2)}) collective-permute-start(f32[64,16,128]{2,0,1:T(8,128)S(1)} %broadcast_select_fusion.1), channel_id=1, source_target_pairs={{0,28},{1,29},{2,30},{3,31},{4,0},{5,1},{6,2},{7,3},{8,4},{9,5},{1... | collective-permute-start | bytes 1572872 | tf_op jit(solution)/shard_map/ppermute | solution.py:16
  124.4 25.5 %collective-permute-start.3 = (f32[64,16,128]{2,0,1:T(8,128)S(1)}, f32[64,16,128]{2,0,1:T(8,128)S(1)}, u32[]{:S(2)}, u32[]{:S(2)}) collective-permute-start(f32[64,16,128]{2,0,1:T(8,128)S(1)} %broadcast_select_fusion.7), channel_id=1, source_target_pairs={{0,24},{1,25},{2,26},{3,27},{4,28},{5,29},{6,30},{7,31},{8,0},{9,1... | collective-permute-start | bytes 1572872 | tf_op jit(solution)/shard_map/ppermute | solution.py:16
  126.5 25.6 %collective-permute-start.10 = (f32[64,16,128]{2,0,1:T(8,128)S(1)}, f32[64,16,128]{2,0,1:T(8,128)S(1)}, u32[]{:S(2)}, u32[]{:S(2)}) collective-permute-start(f32[64,16,128]{2,0,1:T(8,128)S(1)} %broadcast_select_fusion.2), channel_id=1, source_target_pairs={{0,2},{1,3},{2,4},{3,5},{4,6},{5,7},{6,8},{7,9},{8,10},{9,11},{10,... | collective-permute-start | bytes 1572872 | tf_op jit(solution)/shard_map/ppermute | solution.py:16
  150.0 28.5 %copy-start.4 = (f32[8,2,1,16384]{3,2,1,0:T(1,128)S(1)}, f32[8,2,1,16384]{3,2,1,0:T(1,128)}, u32[]{:S(2)}) copy-start(f32[8,2,1,16384]{3,2,1,0:T(1,128)} %param.11) | copy-start | bytes 3145732
  150.0 33.8 %collective-permute-start.4 = (f32[64,16,128]{2,0,1:T(8,128)S(1)}, f32[64,16,128]{2,0,1:T(8,128)S(1)}, u32[]{:S(2)}, u32[]{:S(2)}) collective-permute-start(f32[64,16,128]{2,0,1:T(8,128)S(1)} %broadcast_select_fusion.8), channel_id=1, source_target_pairs={{0,16},{1,17},{2,18},{3,19},{4,20},{5,21},{6,22},{7,23},{8,24},{9,... | collective-permute-start | bytes 1572872 | tf_op jit(solution)/shard_map/ppermute | solution.py:16
  152.3 41.7 %collective-permute-start.11 = (f32[64,16,128]{2,0,1:T(8,128)S(1)}, f32[64,16,128]{2,0,1:T(8,128)}, u32[]{:S(2)}, u32[]{:S(2)}) collective-permute-start(f32[64,16,128]{2,0,1:T(8,128)S(1)} %broadcast_select_fusion.3), channel_id=1, source_target_pairs={{0,1},{1,2},{2,3},{3,4},{4,5},{5,6},{6,7},{7,8},{8,9},{9,10},{10,1... | collective-permute-start | bytes 1572872 | tf_op jit(solution)/shard_map/ppermute | solution.py:16
  180.3 25.4 %all-to-all-start = ((f32[8,2,128,128]{3,1,0,2:T(2,128)}), f32[8,2,128,128]{3,1,0,2:T(2,128)S(1)}, u32[]{:S(2)}, u32[]{:S(2)}) async-start(f32[8,2,128,128]{3,1,0,2:T(2,128)} %copy.37), calls=%async_computation | async-start | bytes 2097152 | tf_op jit(solution)/shard_map/all_to_all | solution.py:60
  184.0 31.9 %collective-permute-start.5 = (f32[64,16,128]{2,0,1:T(8,128)S(1)}, f32[64,16,128]{2,0,1:T(8,128)S(1)}, u32[]{:S(2)}, u32[]{:S(2)}) collective-permute-start(f32[64,16,128]{2,0,1:T(8,128)S(1)} %broadcast_select_fusion.9), channel_id=1, source_target_pairs={{0,31},{1,0},{2,1},{3,2},{4,3},{5,4},{6,5},{7,6},{8,7},{9,8},{10,9... | collective-permute-start | bytes 1572872 | tf_op jit(solution)/shard_map/ppermute | solution.py:16
  185.7 30.2 %collective-permute-start.6 = (f32[64,16,128]{2,0,1:T(8,128)S(1)}, f32[64,16,128]{2,0,1:T(8,128)}, u32[]{:S(2)}, u32[]{:S(2)}) collective-permute-start(f32[64,16,128]{2,0,1:T(8,128)S(1)} %broadcast_select_fusion.9), channel_id=1, source_target_pairs={{0,1},{1,2},{2,3},{3,4},{4,5},{5,6},{6,7},{7,8},{8,9},{9,10},{10,1... | collective-permute-start | bytes 1572872 | tf_op jit(solution)/shard_map/ppermute | solution.py:16
  195.1 30.9 %collective-permute-start.12 = (f32[64,16,128]{2,0,1:T(8,128)S(1)}, f32[64,16,128]{2,0,1:T(8,128)S(1)}, u32[]{:S(2)}, u32[]{:S(2)}) collective-permute-start(f32[64,16,128]{2,0,1:T(8,128)S(1)} %broadcast_select_fusion.4), channel_id=1, source_target_pairs={{0,31},{1,0},{2,1},{3,2},{4,3},{5,4},{6,5},{7,6},{8,7},{9,8},{10,9... | collective-permute-start | bytes 1572872 | tf_op jit(solution)/shard_map/ppermute | solution.py:16
  200.6 25.4 %collective-permute-start.13 = (f32[64,16,128]{2,0,1:T(8,128)S(1)}, f32[64,16,128]{2,0,1:T(8,128)}, u32[]{:S(2)}, u32[]{:S(2)}) collective-permute-start(f32[64,16,128]{2,0,1:T(8,128)S(1)} %broadcast_select_fusion.4), channel_id=1, source_target_pairs={{0,1},{1,2},{2,3},{3,4},{4,5},{5,6},{6,7},{7,8},{8,9},{9,10},{10,1... | collective-permute-start | bytes 1572872 | tf_op jit(solution)/shard_map/ppermute | solution.py:16
  246.2 1.2 copy-start.3
where the time goes:
time: 250 us
  starting transfers between devices  95.6 us (38%)
  waiting for transfers between devices  83.4 us (33%)
  blocking collectives  50.5 us (20%)
  local copies, waits for them, and re-layouts  10.1 us (4%)
  other arithmetic  6.77 us (3%)
  matrix products  2.96 us (1%)
    ppermute x14, starting transfers between devices, shifted(): return lax.ppermute(value, axis, pairs)  84.5 us
    ppermute x14, waiting for transfers between devices, shifted(): return lax.ppermute(value, axis, pairs)  78.3 us
    all_gather x1, blocking collectives, body(): small = lax.all_gather(small, 'tm', tiled=True).astype(jnp.int32)  34 us
    all_to_all x1, blocking collectives, body(): lax.all_to_all(summed, 'tm', split_axis=0, concat_axis=2, tiled=True)  16.5 us
    all_to_all x1, starting transfers between devices, body(): lax.all_to_all(rotor_coeffs.reshape(local_c, comp, rows, LANES), 'tm', sp...  7.48 us
    all_to_all x1, waiting for transfers between devices, body(): lax.all_to_all(mortar_weights.reshape(local_j, sten, rows, LANES), 'tm',...  5.02 us
  transfers between devices with their start and end apart: 16, of which 10 were waited for; matrix products, arithmetic and copies ran while one was open for 3% of the time, Pallas kernels for 0%

commit v1 on v0

--- a/solution.py
+++ b/solution.py
@@ -65,7 +65,9 @@
         tiled=True,
     )
     small = jnp.concatenate([block_shifts[:, None], stencil_offsets], axis=1).astype(jnp.float32)
-    small = lax.all_gather(small, "tm", tiled=True).astype(jnp.int32)
+    small = jnp.concatenate(
+        lax.all_to_all(jnp.stack([small] * lax.axis_size("tm")), "tm", 0, 0), axis=0
+    ).astype(jnp.int32)
     shifts, offsets = (small[:, 0], small[:, 1:])
     gain = lax.dynamic_slice_in_dim(
         reluctivity.reshape(rows, LANES), lax.axis_index("tm") * chunk, chunk, axis=0

time: 250 us -> 237 us (0.948)
  blocking collectives: 50.5 us -> 18.2 us
  waiting for transfers between devices: 83.4 us -> 99 us
  starting transfers between devices: 95.6 us -> 98.2 us
    all_gather x1 -> x0, blocking collectives: 34 us -> none  [body(): small = lax.all_gather(small, 'tm', tiled=True).astype(jnp.int32)]
    all_to_all x1, waiting for transfers between devices: 0.01 us -> 12.8 us  [body(): lax.all_to_all(rotor_coeffs.reshape(local_c, comp, rows, LANES), 'tm', sp...]
    all_to_all x0 -> x1, starting transfers between devices: none -> 7.48 us  [body(): lax.all_to_all(jnp.stack([small] * lax.axis_size('tm')), 'tm', 0, 0)]
    all_to_all x1, starting transfers between devices: 7.48 us -> 3.56 us  [body(): lax.all_to_all(rotor_coeffs.reshape(local_c, comp, rows, LANES), 'tm', sp...]
    all_to_all x0 -> x1, waiting for transfers between devices: none -> 3.57 us  [body(): lax.all_to_all(jnp.stack([small] * lax.axis_size('tm')), 'tm', 0, 0)]
  transfers between devices with their start and end apart: 16 -> 17, of which waited for: 10 -> 12; matrix products, arithmetic and copies ran while one was open for 3% -> 4% of each run, Pallas kernels for 0% -> 0%
where the time goes in v1:
time: 237 us; the launch traced here: 236 us
  waiting for transfers between devices  99 us (42%)
  starting transfers between devices  98.2 us (41%)
  blocking collectives  18.2 us (8%)
  local copies, waits for them, and re-layouts  10.7 us (5%)
  other arithmetic  6.77 us (3%)
  matrix products  2.96 us (1%)
    ppermute x14, starting transfers between devices, shifted(): return lax.ppermute(value, axis, pairs)  83.6 us
    ppermute x14, waiting for transfers between devices, shifted(): return lax.ppermute(value, axis, pairs)  77.6 us
    all_to_all x1, blocking collectives, body(): lax.all_to_all(summed, 'tm', split_axis=0, concat_axis=2, tiled=True)  18.2 us
    all_to_all x1, waiting for transfers between devices, body(): lax.all_to_all(rotor_coeffs.reshape(local_c, comp, rows, LANES), 'tm', sp...  12.8 us
    all_to_all x1, starting transfers between devices, body(): lax.all_to_all(jnp.stack([small] * lax.axis_size('tm')), 'tm', 0, 0)  7.48 us
    all_to_all x1, waiting for transfers between devices, body(): lax.all_to_all(mortar_weights.reshape(local_j, sten, rows, LANES), 'tm',...  5.04 us
  transfers between devices with their start and end apart: 17, of which 12 were waited for; matrix products, arithmetic and copies ran while one was open for 4% of the time, Pallas kernels for 0%

profile of v1, /device:TPU:1, one launch (start us, length us, event | category | flops | bytes accessed | tf_op | source)
XLA Modules:
  0.0 236.2 jit_solution(2325139877974604203)
XLA Ops:
  1.3 7.5 %all-to-all-start.1 = ((f32[8,8,3]{1,2,0:T(4,128)}), f32[8,8,3]{1,2,0:T(4,128)S(1)}, u32[]{:S(2)}, u32[]{:S(2)}) async-start(f32[8,8,3]{1,2,0:T(4,128)} %stack.8), calls=%async_computation.1 | async-start | bytes 32768 | tf_op jit(solution)/shard_map/all_to_all | solution.py:69
  8.8 3.0 %copy.40 = f32[8,2,128,128]{3,1,0,2:T(2,128)} copy(f32[8,2,128,128]{3,2,1,0:T(8,128)} %bitcast.71) | data formatting | bytes 2097152 | tf_op jit(solution)/shard_map/reshape | solution.py:54
  11.8 3.6 %all-to-all-done.1 = f32[8,8,3]{1,2,0:T(4,128)S(1)} async-done(((f32[8,8,3]{1,2,0:T(4,128)}), f32[8,8,3]{1,2,0:T(4,128)S(1)}, u32[]{:S(2)}, u32[]{:S(2)}) %all-to-all-start.1) | async-done | bytes 800 | tf_op jit(solution)/shard_map/all_to_all | solution.py:69
  15.4 3.6 %all-to-all-start.2 = ((f32[8,2,128,128]{3,1,0,2:T(2,128)}), f32[8,2,128,128]{3,1,0,2:T(2,128)S(1)}, u32[]{:S(2)}, u32[]{:S(2)}) async-start(f32[8,2,128,128]{3,1,0,2:T(2,128)} %copy.40), calls=%async_computation.2 | async-start | bytes 2097152 | tf_op jit(solution)/shard_map/all_to_all | solution.py:53
  19.1 12.8 %all-to-all-done.2 = f32[8,2,128,128]{3,1,0,2:T(2,128)S(1)} async-done(((f32[8,2,128,128]{3,1,0,2:T(2,128)}), f32[8,2,128,128]{3,1,0,2:T(2,128)S(1)}, u32[]{:S(2)}, u32[]{:S(2)}) %all-to-all-start.2) | async-done | bytes 1048608 | tf_op jit(solution)/shard_map/all_to_all | solution.py:53
  32.2 1.8 fusion
  34.1 4.1 %collective-permute-start = (f32[64,16,128]{2,0,1:T(8,128)S(1)}, f32[64,16,128]{2,0,1:T(8,128)S(1)}, u32[]{:S(2)}, u32[]{:S(2)}) collective-permute-start(f32[64,16,128]{2,0,1:T(8,128)S(1)} %get-tuple-element.22), channel_id=1, source_target_pairs={{0,1},{1,2},{2,3},{3,4},{4,5},{5,6},{6,7},{7,8},{8,9},{9,10},{10,1... | collective-permute-start | bytes 1572872 | tf_op jit(solution)/shard_map/ppermute | solution.py:16
  38.2 6.9 %collective-permute-start.7 = (f32[64,16,128]{2,0,1:T(8,128)S(1)}, f32[64,16,128]{2,0,1:T(8,128)S(1)}, u32[]{:S(2)}, u32[]{:S(2)}) collective-permute-start(f32[64,16,128]{2,0,1:T(8,128)S(1)} %get-tuple-element.23), channel_id=1, source_target_pairs={{0,16},{1,17},{2,18},{3,19},{4,20},{5,21},{6,22},{7,23},{8,24},{9,... | collective-permute-start | bytes 1572872 | tf_op jit(solution)/shard_map/ppermute | solution.py:16
  47.0 12.8 %collective-permute-done.7 = f32[64,16,128]{2,0,1:T(8,128)S(1)} collective-permute-done((f32[64,16,128]{2,0,1:T(8,128)S(1)}, f32[64,16,128]{2,0,1:T(8,128)S(1)}, u32[]{:S(2)}, u32[]{:S(2)}) %collective-permute-start.7) | collective-permute-done | bytes 524320 | tf_op jit(solution)/shard_map/ppermute | solution.py:16
  59.9 7.1 %collective-permute-start.1 = (f32[64,16,128]{2,0,1:T(8,128)S(1)}, f32[64,16,128]{2,0,1:T(8,128)S(1)}, u32[]{:S(2)}, u32[]{:S(2)}) collective-permute-start(f32[64,16,128]{2,0,1:T(8,128)S(1)} %get-tuple-element.20), channel_id=1, source_target_pairs={{0,2},{1,3},{2,4},{3,5},{4,6},{5,7},{6,8},{7,9},{8,10},{9,11},{10,... | collective-permute-start | bytes 1572872 | tf_op jit(solution)/shard_map/ppermute | solution.py:16
  67.0 9.6 %collective-permute-start.8 = (f32[64,16,128]{2,0,1:T(8,128)S(1)}, f32[64,16,128]{2,0,1:T(8,128)S(1)}, u32[]{:S(2)}, u32[]{:S(2)}) collective-permute-start(f32[64,16,128]{2,0,1:T(8,128)S(1)} %get-tuple-element.21), channel_id=1, source_target_pairs={{0,8},{1,9},{2,10},{3,11},{4,12},{5,13},{6,14},{7,15},{8,16},{9,17... | collective-permute-start | bytes 1572872 | tf_op jit(solution)/shard_map/ppermute | solution.py:16
  76.7 8.9 %collective-permute-done.1 = f32[64,16,128]{2,0,1:T(8,128)S(1)} collective-permute-done((f32[64,16,128]{2,0,1:T(8,128)S(1)}, f32[64,16,128]{2,0,1:T(8,128)S(1)}, u32[]{:S(2)}, u32[]{:S(2)}) %collective-permute-start.1) | collective-permute-done | bytes 524320 | tf_op jit(solution)/shard_map/ppermute | solution.py:16
  86.8 11.3 %collective-permute-done.8 = f32[64,16,128]{2,0,1:T(8,128)S(1)} collective-permute-done((f32[64,16,128]{2,0,1:T(8,128)S(1)}, f32[64,16,128]{2,0,1:T(8,128)S(1)}, u32[]{:S(2)}, u32[]{:S(2)}) %collective-permute-start.8) | collective-permute-done | bytes 524320 | tf_op jit(solution)/shard_map/ppermute | solution.py:16
  98.3 11.0 %collective-permute-done.2 = f32[64,16,128]{2,0,1:T(8,128)S(1)} collective-permute-done((f32[64,16,128]{2,0,1:T(8,128)S(1)}, f32[64,16,128]{2,0,1:T(8,128)S(1)}, u32[]{:S(2)}, u32[]{:S(2)}) %collective-permute-start.2) | collective-permute-done | bytes 524320 | tf_op jit(solution)/shard_map/ppermute | solution.py:16
  111.5 10.6 %collective-permute-start.10 = (f32[64,16,128]{2,0,1:T(8,128)S(1)}, f32[64,16,128]{2,0,1:T(8,128)S(1)}, u32[]{:S(2)}, u32[]{:S(2)}) collective-permute-start(f32[64,16,128]{2,0,1:T(8,128)S(1)} %broadcast_select_fusion.2), channel_id=1, source_target_pairs={{0,2},{1,3},{2,4},{3,5},{4,6},{5,7},{6,8},{7,9},{8,10},{9,11},{10,... | collective-permute-start | bytes 1572872 | tf_op jit(solution)/shard_map/ppermute | solution.py:16
  122.1 12.8 %collective-permute-done.3 = f32[64,16,128]{2,0,1:T(8,128)S(1)} collective-permute-done((f32[64,16,128]{2,0,1:T(8,128)S(1)}, f32[64,16,128]{2,0,1:T(8,128)S(1)}, u32[]{:S(2)}, u32[]{:S(2)}) %collective-permute-start.3) | collective-permute-done | bytes 524320 | tf_op jit(solution)/shard_map/ppermute | solution.py:16
  135.1 2.0 collective-permute-start.4
  137.2 26.1 %collective-permute-start.11 = (f32[64,16,128]{2,0,1:T(8,128)S(1)}, f32[64,16,128]{2,0,1:T(8,128)}, u32[]{:S(2)}, u32[]{:S(2)}) collective-permute-start(f32[64,16,128]{2,0,1:T(8,128)S(1)} %broadcast_select_fusion.3), channel_id=1, source_target_pairs={{0,1},{1,2},{2,3},{3,4},{4,5},{5,6},{6,7},{7,8},{8,9},{9,10},{10,1... | collective-permute-start | bytes 1572872 | tf_op jit(solution)/shard_map/ppermute | solution.py:16
  163.3 1.8 copy.35
  165.1 3.6 %all-to-all-start = ((f32[8,2,128,128]{3,1,0,2:T(2,128)}), f32[8,2,128,128]{3,1,0,2:T(2,128)S(1)}, u32[]{:S(2)}, u32[]{:S(2)}) async-start(f32[8,2,128,128]{3,1,0,2:T(2,128)} %copy.35), calls=%async_computation | async-start | bytes 2097152 | tf_op jit(solution)/shard_map/all_to_all | solution.py:60
  168.8 1.8 collective-permute-start.5
  170.7 6.9 %collective-permute-start.6 = (f32[64,16,128]{2,0,1:T(8,128)S(1)}, f32[64,16,128]{2,0,1:T(8,128)}, u32[]{:S(2)}, u32[]{:S(2)}) collective-permute-start(f32[64,16,128]{2,0,1:T(8,128)S(1)} %broadcast_select_fusion.9), channel_id=1, source_target_pairs={{0,1},{1,2},{2,3},{3,4},{4,5},{5,6},{6,7},{7,8},{8,9},{9,10},{10,1... | collective-permute-start | bytes 1572872 | tf_op jit(solution)/shard_map/ppermute | solution.py:16
  178.1 1.2 broadcast_select_fusion.4
  179.3 6.3 %collective-permute-start.12 = (f32[64,16,128]{2,0,1:T(8,128)S(1)}, f32[64,16,128]{2,0,1:T(8,128)S(1)}, u32[]{:S(2)}, u32[]{:S(2)}) collective-permute-start(f32[64,16,128]{2,0,1:T(8,128)S(1)} %broadcast_select_fusion.4), channel_id=1, source_target_pairs={{0,31},{1,0},{2,1},{3,2},{4,3},{5,4},{6,5},{7,6},{8,7},{9,8},{10,9... | collective-permute-start | bytes 1572872 | tf_op jit(solution)/shard_map/ppermute | solution.py:16
  185.6 5.0 %all-to-all-done = f32[8,2,128,128]{3,1,0,2:T(2,128)S(1)} async-done(((f32[8,2,128,128]{3,1,0,2:T(2,128)}), f32[8,2,128,128]{3,1,0,2:T(2,128)S(1)}, u32[]{:S(2)}, u32[]{:S(2)}) %all-to-all-start) | async-done | bytes 1048608 | tf_op jit(solution)/shard_map/all_to_all | solution.py:60
  191.6 8.8 %collective-permute-done.5 = f32[64,16,128]{2,0,1:T(8,128)S(1)} collective-permute-done((f32[64,16,128]{2,0,1:T(8,128)S(1)}, f32[64,16,128]{2,0,1:T(8,128)S(1)}, u32[]{:S(2)}, u32[]{:S(2)}) %collective-permute-start.5) | collective-permute-done | bytes 524320 | tf_op jit(solution)/shard_map/ppermute | solution.py:16
  200.4 10.5 %collective-permute-done.12 = f32[64,16,128]{2,0,1:T(8,128)S(1)} collective-permute-done((f32[64,16,128]{2,0,1:T(8,128)S(1)}, f32[64,16,128]{2,0,1:T(8,128)S(1)}, u32[]{:S(2)}, u32[]{:S(2)}) %collective-permute-start.12) | collective-permute-done | bytes 524320 | tf_op jit(solution)/shard_map/ppermute | solution.py:16
  210.9 1.7 add_bitcast_fusion.1
  212.8 1.2 fusion.3
  214.7 18.2 %all_to_all.56 = f32[64,2,16,128]{3,2,1,0:T(8,128)S(1)} all-to-all(f32[64,2,16,128]{3,2,1,0:T(8,128)S(1)} %copy.44), channel_id=1, replica_groups=mesh['tm'=8,'azim'=32] {'tm'}, dimensions={0} | all-to-all | bytes 2097152 | tf_op jit(solution)/shard_map/all_to_all | solution.py:99
  233.0 1.1 copy-done.3
  234.1 2.1 sub.12
  (54 shorter events, 10.3 us)
Async XLA Ops:
  0.0 185.6 %copy-start = (f32[1,16384]{1,0:T(1,128)S(1)}, f32[1,16384]{1,0:T(1,128)}, u32[]{:S(2)}) copy-start(f32[1,16384]{1,0:T(1,128)} %param.14) | copy-start | bytes 196612
  0.0 0.7 copy-start.5
  0.0 0.7 copy-start.6
  1.3 14.1 %all-to-all-start.1 = ((f32[8,8,3]{1,2,0:T(4,128)}), f32[8,8,3]{1,2,0:T(4,128)S(1)}, u32[]{:S(2)}, u32[]{:S(2)}) async-start(f32[8,8,3]{1,2,0:T(4,128)} %stack.8), calls=%async_computation.1 | async-start | bytes 32768 | tf_op jit(solution)/shard_map/all_to_all | solution.py:69
  15.4 16.5 %all-to-all-start.2 = ((f32[8,2,128,128]{3,1,0,2:T(2,128)}), f32[8,2,128,128]{3,1,0,2:T(2,128)S(1)}, u32[]{:S(2)}, u32[]{:S(2)}) async-start(f32[8,2,128,128]{3,1,0,2:T(2,128)} %copy.40), calls=%async_computation.2 | async-start | bytes 2097152 | tf_op jit(solution)/shard_map/all_to_all | solution.py:53
  34.0 11.2 %copy-start.1 = (s32[32,5]{1,0:T(8,128)S(1)}, s32[32,5]{1,0:T(8,128)}, u32[]{:S(2)}) copy-start(s32[32,5]{1,0:T(8,128)} %constant.99.clone2.1) | copy-start | bytes 1924
  34.1 12.8 %collective-permute-start = (f32[64,16,128]{2,0,1:T(8,128)S(1)}, f32[64,16,128]{2,0,1:T(8,128)S(1)}, u32[]{:S(2)}, u32[]{:S(2)}) collective-permute-start(f32[64,16,128]{2,0,1:T(8,128)S(1)} %get-tuple-element.22), channel_id=1, source_target_pairs={{0,1},{1,2},{2,3},{3,4},{4,5},{5,6},{6,7},{7,8},{8,9},{9,10},{10,1... | collective-permute-start | bytes 1572872 | tf_op jit(solution)/shard_map/ppermute | solution.py:16
  38.2 21.5 %collective-permute-start.7 = (f32[64,16,128]{2,0,1:T(8,128)S(1)}, f32[64,16,128]{2,0,1:T(8,128)S(1)}, u32[]{:S(2)}, u32[]{:S(2)}) collective-permute-start(f32[64,16,128]{2,0,1:T(8,128)S(1)} %get-tuple-element.23), channel_id=1, source_target_pairs={{0,16},{1,17},{2,18},{3,19},{4,20},{5,21},{6,22},{7,23},{8,24},{9,... | collective-permute-start | bytes 1572872 | tf_op jit(solution)/shard_map/ppermute | solution.py:16
  45.2 0.7 copy-start.2
  59.9 25.6 %collective-permute-start.1 = (f32[64,16,128]{2,0,1:T(8,128)S(1)}, f32[64,16,128]{2,0,1:T(8,128)S(1)}, u32[]{:S(2)}, u32[]{:S(2)}) collective-permute-start(f32[64,16,128]{2,0,1:T(8,128)S(1)} %get-tuple-element.20), channel_id=1, source_target_pairs={{0,2},{1,3},{2,4},{3,5},{4,6},{5,7},{6,8},{7,9},{8,10},{9,11},{10,... | collective-permute-start | bytes 1572872 | tf_op jit(solution)/shard_map/ppermute | solution.py:16
  67.0 31.1 %collective-permute-start.8 = (f32[64,16,128]{2,0,1:T(8,128)S(1)}, f32[64,16,128]{2,0,1:T(8,128)S(1)}, u32[]{:S(2)}, u32[]{:S(2)}) collective-permute-start(f32[64,16,128]{2,0,1:T(8,128)S(1)} %get-tuple-element.21), channel_id=1, source_target_pairs={{0,8},{1,9},{2,10},{3,11},{4,12},{5,13},{6,14},{7,15},{8,16},{9,17... | collective-permute-start | bytes 1572872 | tf_op jit(solution)/shard_map/ppermute | solution.py:16
  85.7 23.6 %collective-permute-start.2 = (f32[64,16,128]{2,0,1:T(8,128)S(1)}, f32[64,16,128]{2,0,1:T(8,128)S(1)}, u32[]{:S(2)}, u32[]{:S(2)}) collective-permute-start(f32[64,16,128]{2,0,1:T(8,128)S(1)} %broadcast_select_fusion.6), channel_id=1, source_target_pairs={{0,4},{1,5},{2,6},{3,7},{4,8},{5,9},{6,10},{7,11},{8,12},{9,13},{1... | collective-permute-start | bytes 1572872 | tf_op jit(solution)/shard_map/ppermute | solution.py:16
  98.2 13.1 %collective-permute-start.9 = (f32[64,16,128]{2,0,1:T(8,128)S(1)}, f32[64,16,128]{2,0,1:T(8,128)S(1)}, u32[]{:S(2)}, u32[]{:S(2)}) collective-permute-start(f32[64,16,128]{2,0,1:T(8,128)S(1)} %broadcast_select_fusion.1), channel_id=1, source_target_pairs={{0,28},{1,29},{2,30},{3,31},{4,0},{5,1},{6,2},{7,3},{8,4},{9,5},{1... | collective-permute-start | bytes 1572872 | tf_op jit(solution)/shard_map/ppermute | solution.py:16
  109.4 25.5 %collective-permute-start.3 = (f32[64,16,128]{2,0,1:T(8,128)S(1)}, f32[64,16,128]{2,0,1:T(8,128)S(1)}, u32[]{:S(2)}, u32[]{:S(2)}) collective-permute-start(f32[64,16,128]{2,0,1:T(8,128)S(1)} %broadcast_select_fusion.7), channel_id=1, source_target_pairs={{0,24},{1,25},{2,26},{3,27},{4,28},{5,29},{6,30},{7,31},{8,0},{9,1... | collective-permute-start | bytes 1572872 | tf_op jit(solution)/shard_map/ppermute | solution.py:16
  111.5 25.6 %collective-permute-start.10 = (f32[64,16,128]{2,0,1:T(8,128)S(1)}, f32[64,16,128]{2,0,1:T(8,128)S(1)}, u32[]{:S(2)}, u32[]{:S(2)}) collective-permute-start(f32[64,16,128]{2,0,1:T(8,128)S(1)} %broadcast_select_fusion.2), channel_id=1, source_target_pairs={{0,2},{1,3},{2,4},{3,5},{4,6},{5,7},{6,8},{7,9},{8,10},{9,11},{10,... | collective-permute-start | bytes 1572872 | tf_op jit(solution)/shard_map/ppermute | solution.py:16
  135.0 28.3 %copy-start.4 = (f32[8,2,1,16384]{3,2,1,0:T(1,128)S(1)}, f32[8,2,1,16384]{3,2,1,0:T(1,128)}, u32[]{:S(2)}) copy-start(f32[8,2,1,16384]{3,2,1,0:T(1,128)} %param.11) | copy-start | bytes 3145732
  135.1 33.6 %collective-permute-start.4 = (f32[64,16,128]{2,0,1:T(8,128)S(1)}, f32[64,16,128]{2,0,1:T(8,128)S(1)}, u32[]{:S(2)}, u32[]{:S(2)}) collective-permute-start(f32[64,16,128]{2,0,1:T(8,128)S(1)} %broadcast_select_fusion.8), channel_id=1, source_target_pairs={{0,16},{1,17},{2,18},{3,19},{4,20},{5,21},{6,22},{7,23},{8,24},{9,... | collective-permute-start | bytes 1572872 | tf_op jit(solution)/shard_map/ppermute | solution.py:16
  137.2 40.9 %collective-permute-start.11 = (f32[64,16,128]{2,0,1:T(8,128)S(1)}, f32[64,16,128]{2,0,1:T(8,128)}, u32[]{:S(2)}, u32[]{:S(2)}) collective-permute-start(f32[64,16,128]{2,0,1:T(8,128)S(1)} %broadcast_select_fusion.3), channel_id=1, source_target_pairs={{0,1},{1,2},{2,3},{3,4},{4,5},{5,6},{6,7},{7,8},{8,9},{9,10},{10,1... | collective-permute-start | bytes 1572872 | tf_op jit(solution)/shard_map/ppermute | solution.py:16
  165.1 25.5 %all-to-all-start = ((f32[8,2,128,128]{3,1,0,2:T(2,128)}), f32[8,2,128,128]{3,1,0,2:T(2,128)S(1)}, u32[]{:S(2)}, u32[]{:S(2)}) async-start(f32[8,2,128,128]{3,1,0,2:T(2,128)} %copy.35), calls=%async_computation | async-start | bytes 2097152 | tf_op jit(solution)/shard_map/all_to_all | solution.py:60
  168.8 31.6 %collective-permute-start.5 = (f32[64,16,128]{2,0,1:T(8,128)S(1)}, f32[64,16,128]{2,0,1:T(8,128)S(1)}, u32[]{:S(2)}, u32[]{:S(2)}) collective-permute-start(f32[64,16,128]{2,0,1:T(8,128)S(1)} %broadcast_select_fusion.9), channel_id=1, source_target_pairs={{0,31},{1,0},{2,1},{3,2},{4,3},{5,4},{6,5},{7,6},{8,7},{9,8},{10,9... | collective-permute-start | bytes 1572872 | tf_op jit(solution)/shard_map/ppermute | solution.py:16
  170.7 29.8 %collective-permute-start.6 = (f32[64,16,128]{2,0,1:T(8,128)S(1)}, f32[64,16,128]{2,0,1:T(8,128)}, u32[]{:S(2)}, u32[]{:S(2)}) collective-permute-start(f32[64,16,128]{2,0,1:T(8,128)S(1)} %broadcast_select_fusion.9), channel_id=1, source_target_pairs={{0,1},{1,2},{2,3},{3,4},{4,5},{5,6},{6,7},{7,8},{8,9},{9,10},{10,1... | collective-permute-start | bytes 1572872 | tf_op jit(solution)/shard_map/ppermute | solution.py:16
  179.3 31.6 %collective-permute-start.12 = (f32[64,16,128]{2,0,1:T(8,128)S(1)}, f32[64,16,128]{2,0,1:T(8,128)S(1)}, u32[]{:S(2)}, u32[]{:S(2)}) collective-permute-start(f32[64,16,128]{2,0,1:T(8,128)S(1)} %broadcast_select_fusion.4), channel_id=1, source_target_pairs={{0,31},{1,0},{2,1},{3,2},{4,3},{5,4},{6,5},{7,6},{8,7},{9,8},{10,9... | collective-permute-start | bytes 1572872 | tf_op jit(solution)/shard_map/ppermute | solution.py:16
  185.6 25.3 %collective-permute-start.13 = (f32[64,16,128]{2,0,1:T(8,128)S(1)}, f32[64,16,128]{2,0,1:T(8,128)}, u32[]{:S(2)}, u32[]{:S(2)}) collective-permute-start(f32[64,16,128]{2,0,1:T(8,128)S(1)} %broadcast_select_fusion.4), channel_id=1, source_target_pairs={{0,1},{1,2},{2,3},{3,4},{4,5},{5,6},{6,7},{7,8},{8,9},{9,10},{10,1... | collective-permute-start | bytes 1572872 | tf_op jit(solution)/shard_map/ppermute | solution.py:16
  232.9 1.2 copy-start.3
